TPU v7x, 512 devices: a whole 4x4x16 slice. The times are simulated.
512 devices in a mesh: dp: 16 (over z), feat: 32 (over y, x, core).
Axes of the slice: x: 4, y: 4, z: 16, core: 2. Of those that a mesh axis runs over, the one named last changes fastest.
Arguments:
- earlier: bfloat16 [3, 16384, 10240], P(None, 'feat', 'dp'), may hold values from -6 to 6
- mix_weights: float32 [3], replicated, may hold values from 0.3 to 1
- destinations: int32 [10240], replicated, may hold values from -1 to 8191, as said below
- cotangent: bfloat16 [16384, 8192], P('feat', 'dp'), may hold values from -6 to 6
- right_gate: bfloat16 [128, 128, 128], P('feat'), may hold values from -0.5 to 0.5
- left_gate: bfloat16 [128, 128, 128], P('feat'), may hold values from -0.5 to 0.5
- right_up: bfloat16 [128, 128, 128], P('feat'), may hold values from -0.5 to 0.5
- left_up: bfloat16 [128, 128, 128], P('feat'), may hold values from -0.5 to 0.5
- right_down: bfloat16 [128, 128, 128], P('feat'), may hold values from -0.5 to 0.5
- left_down: bfloat16 [128, 128, 128], P('feat'), may hold values from -0.5 to 0.5
Outputs:
- output: bfloat16 [16384, 8192], P('feat', 'dp')
- mixed_grad: bfloat16 [16384, 10240], P('feat', 'dp')
- grad_right_gate: float32 [128, 128, 128], P('feat', 'dp')
- grad_left_gate: float32 [128, 128, 128], P('feat', 'dp')
- grad_right_up: float32 [128, 128, 128], P('feat', 'dp')
- grad_left_up: float32 [128, 128, 128], P('feat', 'dp')
- grad_right_down: float32 [128, 128, 128], P('feat', 'dp')
- grad_left_down: float32 [128, 128, 128], P('feat', 'dp')
Inputs may be any that keep to these rules, and one draw needn't show every extreme that they name: `destinations`: every packed row 0 to 8191 is named by exactly one slot; other slots hold -1. Among the 640 slots of one index of dp, at most 40 name rows of any one index of dp (packed rows of index g are g * 512 to (g + 1) * 512 - 1). In every draw one index of dp fills all its 640 slots, sending exactly 40 rows to every index.
All inputs are finite; a program needn't handle non-finite values.
Results may differ from a plain program's by a relative error of at most 0.0092.
Values may be sent and summed in bfloat16 or wider, within the bound.
A program may use at most 64 MiB of HBM per device.

v0:
```python
import jax
import jax.numpy as jnp
from jax import lax
from jax.sharding import PartitionSpec as P


def right_apply(values, right_factor):
    return jnp.einsum(
        "ijt,ijo->iot", values, right_factor, preferred_element_type=jnp.float32
    ).astype(jnp.bfloat16)


def left_apply(spread, left_factor):
    return jnp.einsum(
        "iot,oip->pot", spread, left_factor, preferred_element_type=jnp.float32
    ).astype(jnp.bfloat16)


def left_back(out_grad, left_factor):
    return jnp.einsum(
        "pot,oip->iot", out_grad, left_factor, preferred_element_type=jnp.float32
    ).astype(jnp.bfloat16)


def right_back(spread_grad, right_factor):
    return jnp.einsum("iot,ijo->ijt", spread_grad, right_factor, preferred_element_type=jnp.float32)


def left_grad(spread, out_grad):
    return jnp.einsum("iot,pot->oip", spread, out_grad, preferred_element_type=jnp.float32)


def right_grad(values, spread_grad):
    return jnp.einsum("ijt,iot->ijo", values, spread_grad, preferred_element_type=jnp.float32)


def gelu_slope(values):
    return jax.vjp(jax.nn.gelu, values)[1](jnp.ones_like(values))[0]


def mixer_block(inputs, out_grads, factors):
    right_gate, left_gate, right_up, left_up, right_down, left_down = factors
    gate_start = right_apply(inputs, right_gate)
    up_start = right_apply(inputs, right_up)
    pieces = (
        lax.all_to_all(gate_start, "feat", split_axis=1, concat_axis=0, tiled=True),
        lax.all_to_all(up_start, "feat", split_axis=1, concat_axis=0, tiled=True),
    )
    gate_spread = pieces[0]
    up_spread = pieces[1]
    gate_mixed = left_apply(pieces[0], left_gate)
    up_mixed = left_apply(pieces[1], left_up)
    gate_out, up_out = (
        lax.all_to_all(gate_mixed, "feat", split_axis=0, concat_axis=1, tiled=True),
        lax.all_to_all(up_mixed, "feat", split_axis=0, concat_axis=1, tiled=True),
    )
    gate_f = gate_out.astype(jnp.float32)
    up_f = up_out.astype(jnp.float32)
    activated = jax.nn.gelu(gate_f)
    hidden = (activated * up_f).astype(jnp.bfloat16)
    down_start = right_apply(hidden, right_down)
    portion = lax.all_to_all(down_start, "feat", split_axis=1, concat_axis=0, tiled=True)
    down_spread = portion
    down_mixed = left_apply(portion, left_down)
    output = lax.all_to_all(down_mixed, "feat", split_axis=0, concat_axis=1, tiled=True)
    portion = lax.all_to_all(out_grads, "feat", split_axis=1, concat_axis=0, tiled=True)
    down_outgrad = portion
    down_spread_grad = left_back(portion, left_down)
    grad_left_down = left_grad(down_spread, down_outgrad)
    portion = lax.all_to_all(down_spread_grad, "feat", split_axis=0, concat_axis=1, tiled=True)
    hidden_grad = right_back(portion, right_down)
    grad_right_down = right_grad(hidden, portion)
    gate_grad = (hidden_grad * up_f * gelu_slope(gate_f)).astype(jnp.bfloat16)
    up_grad = (hidden_grad * activated).astype(jnp.bfloat16)
    pieces = (
        lax.all_to_all(gate_grad, "feat", split_axis=1, concat_axis=0, tiled=True),
        lax.all_to_all(up_grad, "feat", split_axis=1, concat_axis=0, tiled=True),
    )
    gate_outgrad = pieces[0]
    up_outgrad = pieces[1]
    gate_spread_grad = left_back(pieces[0], left_gate)
    up_spread_grad = left_back(pieces[1], left_up)
    grad_left_gate = left_grad(gate_spread, gate_outgrad)
    grad_left_up = left_grad(up_spread, up_outgrad)
    pieces = (
        lax.all_to_all(gate_spread_grad, "feat", split_axis=0, concat_axis=1, tiled=True),
        lax.all_to_all(up_spread_grad, "feat", split_axis=0, concat_axis=1, tiled=True),
    )
    gate_start_grad = pieces[0]
    up_start_grad = pieces[1]
    input_grad = right_back(pieces[0], right_gate) + right_back(pieces[1], right_up)
    grad_right_gate = right_grad(inputs, gate_start_grad)
    grad_right_up = right_grad(inputs, up_start_grad)
    grads = (
        grad_right_gate,
        grad_left_gate,
        grad_right_up,
        grad_left_up,
        grad_right_down,
        grad_left_down,
    )
    return (output, input_grad.astype(jnp.bfloat16), grads)


def body(
    earlier,
    mix_weights,
    destinations,
    cotangent,
    right_gate,
    left_gate,
    right_up,
    left_up,
    right_down,
    left_down,
):
    factors = (right_gate, left_gate, right_up, left_up, right_down, left_down)
    block_count = right_gate.shape[0]
    block_width = right_gate.shape[1]
    feat_count = earlier.shape[1]
    slot_count = earlier.shape[2]
    tok_rows = cotangent.shape[1]
    groups = lax.axis_size("dp")
    own_index = lax.axis_index("dp")
    cap_rows = 5 * tok_rows // (4 * groups)
    lane_count = groups * cap_rows
    route_table = destinations.reshape(groups, slot_count)
    target = jnp.where(route_table >= 0, route_table // tok_rows, -1)
    members = (target[:, :, None] == jnp.arange(groups, dtype=jnp.int32)[None, None, :]).astype(
        jnp.int32
    )
    places = jnp.sum((jnp.cumsum(members, axis=1) - 1) * members, axis=2)
    mine_target = lax.dynamic_index_in_dim(target, own_index, 0, keepdims=False)
    mine_place = lax.dynamic_index_in_dim(places, own_index, 0, keepdims=False)
    home_index = jnp.where(mine_target >= 0, mine_target * cap_rows + mine_place, lane_count)
    outgoing = (
        jnp.full((lane_count,), slot_count, jnp.int32)
        .at[home_index]
        .set(jnp.arange(slot_count, dtype=jnp.int32), mode="drop")
    )
    arriving = target == own_index
    lane_of = jnp.arange(groups, dtype=jnp.int32)[:, None] * cap_rows + places
    slot_here = route_table - own_index * tok_rows
    incoming = (
        jnp.zeros((tok_rows,), jnp.int32)
        .at[jnp.where(arriving, slot_here, tok_rows)]
        .set(lane_of, mode="drop")
    )
    returning = (
        jnp.full((lane_count,), tok_rows, jnp.int32)
        .at[jnp.where(arriving, lane_of, lane_count)]
        .set(slot_here, mode="drop")
    )
    averaged = jnp.zeros((feat_count, slot_count), jnp.float32)
    for depth_index in range(earlier.shape[0]):
        averaged = averaged + mix_weights[depth_index] * earlier[depth_index].astype(jnp.float32)
    mixed = averaged.astype(jnp.bfloat16)
    lane_data = jnp.take(cotangent, returning, axis=1, mode="fill", fill_value=0)
    received = lax.all_to_all(lane_data, "dp", split_axis=1, concat_axis=1, tiled=True)
    slot_grads = jnp.take(received, home_index, axis=1, mode="fill", fill_value=0)
    result, input_grad, grads = mixer_block(
        mixed.reshape(block_count, block_width, slot_count),
        slot_grads.reshape(block_count, block_width, slot_count),
        factors,
    )
    lane_data = jnp.take(
        result.reshape(feat_count, slot_count), outgoing, axis=1, mode="fill", fill_value=0
    )
    received = lax.all_to_all(lane_data, "dp", split_axis=1, concat_axis=1, tiled=True)
    output = jnp.take(received, incoming, axis=1)
    mixed_grad = input_grad.reshape(feat_count, slot_count)
    summed = (
        lax.psum_scatter(grads[0], "dp", scatter_dimension=1, tiled=True),
        lax.psum_scatter(grads[1], "dp", scatter_dimension=1, tiled=True),
        lax.psum_scatter(grads[2], "dp", scatter_dimension=1, tiled=True),
        lax.psum_scatter(grads[3], "dp", scatter_dimension=1, tiled=True),
        lax.psum_scatter(grads[4], "dp", scatter_dimension=1, tiled=True),
        lax.psum_scatter(grads[5], "dp", scatter_dimension=1, tiled=True),
    )
    grad_scale = (tok_rows * groups) ** (-0.5)
    return (
        output,
        mixed_grad,
        summed[0] * grad_scale,
        summed[1] * grad_scale,
        summed[2] * grad_scale,
        summed[3] * grad_scale,
        summed[4] * grad_scale,
        summed[5] * grad_scale,
    )


def solution(mesh):
    return jax.shard_map(
        body,
        mesh=mesh,
        in_specs=(
            P(None, "feat", "dp"),
            P(),
            P(),
            P("feat", "dp"),
            P("feat", None, None),
            P("feat", None, None),
            P("feat", None, None),
            P("feat", None, None),
            P("feat", None, None),
            P("feat", None, None),
        ),
        out_specs=(
            P("feat", "dp"),
            P("feat", "dp"),
            P("feat", "dp", None),
            P("feat", "dp", None),
            P("feat", "dp", None),
            P("feat", "dp", None),
            P("feat", "dp", None),
            P("feat", "dp", None),
        ),
        check_vma=False,
    )
```

profile of v0, /device:TPU:1, one launch (start us, length us, event | category | flops | bytes accessed | tf_op | source)
XLA Modules:
  0.0 755.2 jit_solution(657560331342249779)
XLA Ops:
  14.1 10.5 %all-to-all-start.2 = ((bf16[4,128,640]{2,0,1:T(4,128)(2,1)}), bf16[4,128,640]{2,0,1:T(4,128)(2,1)S(1)}, u32[]{:S(2)}, u32[]{:S(2)}) async-start(bf16[4,128,640]{2,0,1:T(4,128)(2,1)} %copy.111), calls=%async_computation.2 | async-start | bytes 1310720 | tf_op jit(solution)/shard_map/all_to_all | solution.py:47
  27.2 22.6 %reduce-window.6 = s32[16,16,5,128]{3,1,2,0:T(8,128)S(1)} reduce-window(s32[16,16,5,128]{3,1,2,0:T(8,128)S(1)} %fusion.20, s32[]{:T(128)} %constant.46.clone.1), window={size=1x1x1x128 pad=0_0x0_0x0_0x127_0}, to_apply=%region_0.1 | reduce-window | flops 20807680 | bytes 1310724 | tf_op jit(solution)/shard_map/reduce-window
  51.8 38.1 %scatter_custom_fusion.2 = s32[640]{0:T(1024)S(1)} fusion(s32[10240]{0:T(1024)S(1)} %reshape.402, s32[10240]{0:T(1024)} %reshape.404, s32[]{:T(128)} %constant.59.clone.1), kind=kCustom, calls=%fused_computation.126 | custom fusion | bytes 3072 | tf_op jit(solution)/shard_map/scatter | solution.py:152
  89.9 7.5 all-to-all-start
  101.6 8.7 %all-to-all-done = bf16[4,128,640]{2,0,1:T(4,128)(2,1)S(1)} async-done(((bf16[4,128,640]{2,0,1:T(4,128)(2,1)}), bf16[4,128,640]{2,0,1:T(4,128)(2,1)S(1)}, u32[]{:S(2)}, u32[]{:S(2)}) %all-to-all-start) | async-done | bytes 655392 | tf_op jit(solution)/shard_map/all_to_all | solution.py:46
  110.3 13.0 %all-to-all-start.7 = ((bf16[512,16,40]{0,2,1:T(8,128)(2,1)}), bf16[512,16,40]{0,2,1:T(8,128)(2,1)S(1)}, u32[]{:S(2)}, u32[]{:S(2)}) async-start(bf16[512,16,40]{0,2,1:T(8,128)(2,1)} %broadcast_select_fusion.1), calls=%async_computation.7 | async-start | bytes 1310720 | tf_op jit(solution)/shard_map/all_to_all | solution.py:159
  126.8 25.4 %all-to-all-done.7 = bf16[512,16,40]{0,2,1:T(8,128)(2,1)S(1)} async-done(((bf16[512,16,40]{0,2,1:T(8,128)(2,1)}), bf16[512,16,40]{0,2,1:T(8,128)(2,1)S(1)}, u32[]{:S(2)}, u32[]{:S(2)}) %all-to-all-start.7) | async-done | bytes 655392 | tf_op jit(solution)/shard_map/all_to_all | solution.py:159
  152.2 10.2 %all-to-all-start.3 = ((bf16[128,4,640]{2,1,0:T(4,128)(2,1)}), bf16[128,4,640]{2,1,0:T(4,128)(2,1)S(1)}, u32[]{:S(2)}, u32[]{:S(2)}) async-start(bf16[128,4,640]{2,1,0:T(4,128)(2,1)} %copy.114), calls=%async_computation.3 | async-start | bytes 1310720 | tf_op jit(solution)/shard_map/all_to_all | solution.py:55
  167.1 8.1 %all-to-all-done.3 = bf16[128,4,640]{2,1,0:T(4,128)(2,1)S(1)} async-done(((bf16[128,4,640]{2,1,0:T(4,128)(2,1)}), bf16[128,4,640]{2,1,0:T(4,128)(2,1)S(1)}, u32[]{:S(2)}, u32[]{:S(2)}) %all-to-all-start.3) | async-done | bytes 655392 | tf_op jit(solution)/shard_map/all_to_all | solution.py:55
  175.2 4.0 all-to-all-start.8
  182.3 9.9 %all-to-all-done.8 = bf16[4,128,640]{2,0,1:T(4,128)(2,1)S(1)} async-done(((bf16[4,128,640]{2,0,1:T(4,128)(2,1)}), bf16[4,128,640]{2,0,1:T(4,128)(2,1)S(1)}, u32[]{:S(2)}, u32[]{:S(2)}) %all-to-all-start.8) | async-done | bytes 655392 | tf_op jit(solution)/shard_map/all_to_all | solution.py:66
  192.2 4.0 all-to-all-start.1
  199.2 10.0 %all-to-all-done.1 = bf16[128,4,640]{2,1,0:T(4,128)(2,1)S(1)} async-done(((bf16[128,4,640]{2,1,0:T(4,128)(2,1)}), bf16[128,4,640]{2,1,0:T(4,128)(2,1)S(1)}, u32[]{:S(2)}, u32[]{:S(2)}) %all-to-all-start.1) | async-done | bytes 655392 | tf_op jit(solution)/shard_map/all_to_all | solution.py:54
  210.0 4.2 all-to-all-start.9
  219.5 7.7 %all-to-all-done.9 = bf16[128,4,640]{2,1,0:T(4,128)(2,1)S(1)} async-done(((bf16[128,4,640]{2,1,0:T(4,128)(2,1)}), bf16[128,4,640]{2,1,0:T(4,128)(2,1)S(1)}, u32[]{:S(2)}, u32[]{:S(2)}) %all-to-all-start.9) | async-done | bytes 655392 | tf_op jit(solution)/shard_map/all_to_all | solution.py:70
  234.4 4.0 all-to-all-start.12
  240.6 10.8 %all-to-all-done.12 = bf16[4,128,640]{2,0,1:T(4,128)(2,1)S(1)} async-done(((bf16[4,128,640]{2,0,1:T(4,128)(2,1)}), bf16[4,128,640]{2,0,1:T(4,128)(2,1)S(1)}, u32[]{:S(2)}, u32[]{:S(2)}) %all-to-all-start.12) | async-done | bytes 655392 | tf_op jit(solution)/shard_map/all_to_all | solution.py:77
  260.5 38.0 %scatter_custom_fusion = s32[512]{0:T(512)S(1)} fusion(s32[10240]{0:T(1024)} %reshape.386, s32[10240]{0:T(1024)} %reshape.388, s32[]{:T(128)} %constant.46.clone.1), kind=kCustom, calls=%fused_computation.131 | custom fusion | bytes 2560 | tf_op jit(solution)/shard_map/scatter | solution.py:147
  298.6 4.1 scatter_custom_fusion.1
  306.1 7.5 all-to-all-start.4
  317.0 9.5 %all-to-all-done.4 = bf16[4,128,640]{2,0,1:T(4,128)(2,1)} async-done(((bf16[4,128,640]{2,0,1:T(4,128)(2,1)}), bf16[4,128,640]{2,0,1:T(4,128)(2,1)}, u32[]{:S(2)}, u32[]{:S(2)}) %all-to-all-start.4) | async-done | bytes 655392 | tf_op jit(solution)/shard_map/all_to_all | solution.py:62
  326.5 4.0 all-to-all-start.13
  337.7 5.9 all-to-all-done.13
  343.5 4.9 all-to-all-start.5
  353.9 7.5 all-to-all-done.5
  361.4 4.0 all-to-all-start.11
  378.4 6.3 all-to-all-start.6
  390.8 72.2 %reduce-scatter.13.cloned.1.call-done = f32[4,8,128]{2,1,0:T(8,128)} async-done(((f32[4,128,128]{2,1,0:T(8,128)}), f32[4,8,128]{2,1,0:T(8,128)}) %reduce-scatter.13.cloned.1.call-update) | async-done | bytes 16400 | tf_op jit(solution)/shard_map/reduce_scatter | solution.py:176
  465.9 68.0 %reduce-scatter.9.cloned.1.call-done = f32[4,8,128]{2,1,0:T(8,128)} async-done(((f32[4,128,128]{2,1,0:T(8,128)}), f32[4,8,128]{2,1,0:T(8,128)}) %reduce-scatter.9.cloned.1.call-update) | async-done | bytes 16400 | tf_op jit(solution)/shard_map/reduce_scatter | solution.py:174
  535.2 68.6 %reduce-scatter.17.cloned.1.call-done = f32[4,8,128]{2,1,0:T(8,128)} async-done(((f32[4,128,128]{2,1,0:T(8,128)}), f32[4,8,128]{2,1,0:T(8,128)}) %reduce-scatter.17.cloned.1.call-update) | async-done | bytes 16400 | tf_op jit(solution)/shard_map/reduce_scatter | solution.py:178
  608.6 64.8 %reduce-scatter.11.cloned.1.call-done = f32[4,8,128]{2,1,0:T(8,128)} async-done(((f32[4,128,128]{2,1,0:T(8,128)}), f32[4,8,128]{2,1,0:T(8,128)}) %reduce-scatter.11.cloned.1.call-update) | async-done | bytes 16400 | tf_op jit(solution)/shard_map/reduce_scatter | solution.py:175
  674.8 69.2 %reduce-scatter.7.cloned.1.call-done = f32[4,8,128]{2,1,0:T(8,128)} async-done(((f32[4,128,128]{2,1,0:T(8,128)}), f32[4,8,128]{2,1,0:T(8,128)}) %reduce-scatter.7.cloned.1.call-update) | async-done | bytes 16400 | tf_op jit(solution)/shard_map/reduce_scatter | solution.py:173
  (186 shorter events, 107.0 us)
Async XLA Ops:
  7.2 222.3 %copy-start = (bf16[4,128,128]{2,1,0:T(8,128)(2,1)S(1)}, bf16[4,128,128]{2,1,0:T(8,128)(2,1)}, u32[]{:S(2)}) copy-start(bf16[4,128,128]{2,1,0:T(8,128)(2,1)} %param.20) | copy-start | bytes 393220
  14.1 75.8 %all-to-all-start.2 = ((bf16[4,128,640]{2,0,1:T(4,128)(2,1)}), bf16[4,128,640]{2,0,1:T(4,128)(2,1)S(1)}, u32[]{:S(2)}, u32[]{:S(2)}) async-start(bf16[4,128,640]{2,0,1:T(4,128)(2,1)} %copy.111), calls=%async_computation.2 | async-start | bytes 1310720 | tf_op jit(solution)/shard_map/all_to_all | solution.py:47
  24.8 26.1 %copy-start.27 = (s32[16,640]{1,0:T(8,128)}, s32[16,640]{1,0:T(8,128)S(1)}, u32[]{:S(2)}) copy-start(s32[16,640]{1,0:T(8,128)S(1)} %get-tuple-element.39) | copy-start | bytes 122884
  50.6 46.8 %copy-start.19 = (bf16[512,512]{1,0:T(8,128)(2,1)S(1)}, bf16[512,512]{1,0:T(8,128)(2,1)}, u32[]{:S(2)}) copy-start(bf16[512,512]{1,0:T(8,128)(2,1)} %param.15) | copy-start | bytes 1572868
  50.8 46.8 %copy-start.29 = (s32[16]{0:T(128)}, s32[16]{0:T(128)S(1)}, u32[]{:S(2)}) copy-start(s32[16]{0:T(128)S(1)} %iota_multiply_fusion) | copy-start | bytes 196
  51.1 72.1 %copy-start.25 = (s32[16,640]{1,0:T(8,128)}, s32[16,640]{1,0:T(8,128)S(1)}, u32[]{:S(2)}) copy-start(s32[16,640]{1,0:T(8,128)S(1)} %fusion.19) | copy-start | bytes 122884
  89.9 20.3 %all-to-all-start = ((bf16[4,128,640]{2,0,1:T(4,128)(2,1)}), bf16[4,128,640]{2,0,1:T(4,128)(2,1)S(1)}, u32[]{:S(2)}, u32[]{:S(2)}) async-start(bf16[4,128,640]{2,0,1:T(4,128)(2,1)} %copy.100), calls=%async_computation | async-start | bytes 1310720 | tf_op jit(solution)/shard_map/all_to_all | solution.py:46
  101.6 23.5 %copy-start.21 = (bf16[4,128,128]{2,1,0:T(8,128)(2,1)S(1)}, bf16[4,128,128]{2,1,0:T(8,128)(2,1)}, u32[]{:S(2)}) copy-start(bf16[4,128,128]{2,1,0:T(8,128)(2,1)} %param.19) | copy-start | bytes 393220
  110.3 41.9 %all-to-all-start.7 = ((bf16[512,16,40]{0,2,1:T(8,128)(2,1)}), bf16[512,16,40]{0,2,1:T(8,128)(2,1)S(1)}, u32[]{:S(2)}, u32[]{:S(2)}) async-start(bf16[512,16,40]{0,2,1:T(8,128)(2,1)} %broadcast_select_fusion.1), calls=%async_computation.7 | async-start | bytes 1310720 | tf_op jit(solution)/shard_map/all_to_all | solution.py:159
  152.2 23.0 %all-to-all-start.3 = ((bf16[128,4,640]{2,1,0:T(4,128)(2,1)}), bf16[128,4,640]{2,1,0:T(4,128)(2,1)S(1)}, u32[]{:S(2)}, u32[]{:S(2)}) async-start(bf16[128,4,640]{2,1,0:T(4,128)(2,1)} %copy.114), calls=%async_computation.3 | async-start | bytes 1310720 | tf_op jit(solution)/shard_map/all_to_all | solution.py:55
  175.2 17.0 %all-to-all-start.8 = ((bf16[4,128,640]{2,0,1:T(4,128)(2,1)}), bf16[4,128,640]{2,0,1:T(4,128)(2,1)S(1)}, u32[]{:S(2)}, u32[]{:S(2)}) async-start(bf16[4,128,640]{2,0,1:T(4,128)(2,1)} %copy.124), calls=%async_computation.8 | async-start | bytes 1310720 | tf_op jit(solution)/shard_map/all_to_all | solution.py:66
  192.2 17.0 %all-to-all-start.1 = ((bf16[128,4,640]{2,1,0:T(4,128)(2,1)}), bf16[128,4,640]{2,1,0:T(4,128)(2,1)S(1)}, u32[]{:S(2)}, u32[]{:S(2)}) async-start(bf16[128,4,640]{2,1,0:T(4,128)(2,1)} %copy.103), calls=%async_computation.1 | async-start | bytes 1310720 | tf_op jit(solution)/shard_map/all_to_all | solution.py:54
  197.8 16.5 %copy-start.16 = (bf16[128,4,640]{2,1,0:T(4,128)(2,1)S(1)}, bf16[128,4,640]{2,1,0:T(4,128)(2,1)}, u32[]{:S(2)}) copy-start(bf16[128,4,640]{2,1,0:T(4,128)(2,1)} %copy-done.15) | copy-start | bytes 1966084
  210.0 17.2 %all-to-all-start.9 = ((bf16[128,4,640]{2,1,0:T(4,128)(2,1)}), bf16[128,4,640]{2,1,0:T(4,128)(2,1)S(1)}, u32[]{:S(2)}, u32[]{:S(2)}) async-start(bf16[128,4,640]{2,1,0:T(4,128)(2,1)} %copy.127), calls=%async_computation.9 | async-start | bytes 1310720 | tf_op jit(solution)/shard_map/all_to_all | solution.py:70
  233.1 69.6 %copy-start.8 = (bf16[4,128,640]{1,2,0:T(8,128)(2,1)}, bf16[4,128,640]{1,2,0:T(8,128)(2,1)S(1)}, u32[]{:S(2)}) copy-start(bf16[4,128,640]{1,2,0:T(8,128)(2,1)S(1)} %get-tuple-element.37) | copy-start | bytes 1966084
  234.4 17.0 %all-to-all-start.12 = ((bf16[4,128,640]{2,0,1:T(4,128)(2,1)}), bf16[4,128,640]{2,0,1:T(4,128)(2,1)S(1)}, u32[]{:S(2)}, u32[]{:S(2)}) async-start(bf16[4,128,640]{2,0,1:T(4,128)(2,1)} %copy.137), calls=%async_computation.12 | async-start | bytes 1310720 | tf_op jit(solution)/shard_map/all_to_all | solution.py:77
  238.4 17.8 %copy-start.30 = (s32[16]{0:T(128)S(1)}, s32[16]{0:T(128)}, u32[]{:S(2)}) copy-start(s32[16]{0:T(128)} %copy-done.29) | copy-start | bytes 196
  252.2 53.9 %all-to-all-start.10 = ((bf16[4,128,640]{2,0,1:T(4,128)(2,1)}), bf16[4,128,640]{2,0,1:T(4,128)(2,1)S(1)}, u32[]{:S(2)}, u32[]{:S(2)}) async-start(bf16[4,128,640]{2,0,1:T(4,128)(2,1)} %copy.132), calls=%async_computation.10 | async-start | bytes 1310720 | tf_op jit(solution)/shard_map/all_to_all | solution.py:76
  306.1 20.4 %all-to-all-start.4 = ((bf16[4,128,640]{2,0,1:T(4,128)(2,1)}), bf16[4,128,640]{2,0,1:T(4,128)(2,1)}, u32[]{:S(2)}, u32[]{:S(2)}) async-start(bf16[4,128,640]{2,0,1:T(4,128)(2,1)} %copy.117), calls=%async_computation.4 | async-start | bytes 1310720 | tf_op jit(solution)/shard_map/all_to_all | solution.py:62
  326.5 17.0 %all-to-all-start.13 = ((bf16[128,4,640]{2,1,0:T(4,128)(2,1)}), bf16[128,4,640]{2,1,0:T(4,128)(2,1)S(1)}, u32[]{:S(2)}, u32[]{:S(2)}) async-start(bf16[128,4,640]{2,1,0:T(4,128)(2,1)} %copy.140), calls=%async_computation.13 | async-start | bytes 1310720 | tf_op jit(solution)/shard_map/all_to_all | solution.py:87
  330.6 58.9 %reduce-scatter.15.cloned.1.call-start = ((), (), s32[]{:S(2)}) async-start(), calls=%async_computation.24 | async-start | bytes 278528 | tf_op jit(solution)/shard_map/reduce_scatter | solution.py:177
  337.7 12.5 %copy-start.2 = (bf16[32,4,4,640]{3,2,1,0:T(4,128)(2,1)S(1)}, bf16[32,4,4,640]{3,2,1,0:T(4,128)(2,1)}, u32[]{:S(2)}) copy-start(bf16[32,4,4,640]{3,2,1,0:T(4,128)(2,1)} %copy-done.1) | copy-start | bytes 1966084
  343.5 17.9 %all-to-all-start.5 = ((bf16[128,4,640]{2,1,0:T(4,128)(2,1)}), bf16[128,4,640]{2,1,0:T(4,128)(2,1)}, u32[]{:S(2)}, u32[]{:S(2)}) async-start(bf16[128,4,640]{2,1,0:T(4,128)(2,1)} %copy.120), calls=%async_computation.5 | async-start | bytes 1310720 | tf_op jit(solution)/shard_map/all_to_all | solution.py:65
  348.4 114.6 %reduce-scatter.13.cloned.1.call-start = ((), (), s32[]{:S(2)}) async-start(), calls=%async_computation.23 | async-start | bytes 278528 | tf_op jit(solution)/shard_map/reduce_scatter | solution.py:176
  352.5 13.0 %copy-start.4 = (bf16[32,4,4,640]{3,2,1,0:T(4,128)(2,1)S(1)}, bf16[32,4,4,640]{3,2,1,0:T(4,128)(2,1)}, u32[]{:S(2)}) copy-start(bf16[32,4,4,640]{3,2,1,0:T(4,128)(2,1)} %copy-done.3) | copy-start | bytes 1966084
  361.4 17.0 %all-to-all-start.11 = ((bf16[128,4,640]{2,1,0:T(4,128)(2,1)}), bf16[128,4,640]{2,1,0:T(4,128)(2,1)S(1)}, u32[]{:S(2)}, u32[]{:S(2)}) async-start(bf16[128,4,640]{2,1,0:T(4,128)(2,1)} %copy.135), calls=%async_computation.11 | async-start | bytes 1310720 | tf_op jit(solution)/shard_map/all_to_all | solution.py:86
  365.5 168.4 %reduce-scatter.9.cloned.1.call-start = ((), (), s32[]{:S(2)}) async-start(), calls=%async_computation.21 | async-start | bytes 278528 | tf_op jit(solution)/shard_map/reduce_scatter | solution.py:174
  378.4 366.8 %all-to-all-start.6 = ((bf16[512,16,40]{0,2,1:T(8,128)(2,1)}), bf16[512,16,40]{0,2,1:T(8,128)(2,1)S(1)}, u32[]{:S(2)}, u32[]{:S(2)}) async-start(bf16[512,16,40]{0,2,1:T(8,128)(2,1)} %bitcast.161), calls=%async_computation.6 | async-start | bytes 1310720 | tf_op jit(solution)/shard_map/all_to_all | solution.py:169
  384.7 219.1 %reduce-scatter.17.cloned.1.call-start = ((), (), s32[]{:S(2)}) async-start(), calls=%async_computation.25 | async-start | bytes 278528 | tf_op jit(solution)/shard_map/reduce_scatter | solution.py:178
  386.9 286.5 %reduce-scatter.11.cloned.1.call-start = ((), (), s32[]{:S(2)}) async-start(), calls=%async_computation.22 | async-start | bytes 278528 | tf_op jit(solution)/shard_map/reduce_scatter | solution.py:175
  464.6 140.6 %copy-start.6 = (bf16[128,4,640]{2,1,0:T(4,128)(2,1)S(1)}, bf16[128,4,640]{2,1,0:T(4,128)(2,1)}, u32[]{:S(2)}) copy-start(bf16[128,4,640]{2,1,0:T(4,128)(2,1)} %copy-done.5) | copy-start | bytes 1966084
  465.9 278.1 %reduce-scatter.7.cloned.1.call-start = ((), (), s32[]{:S(2)}) async-start(), calls=%async_computation.20 | async-start | bytes 278528 | tf_op jit(solution)/shard_map/reduce_scatter | solution.py:173
  (20 other events, 70.2 us)
Sparse Core Ops, SparseCore 0:
  334.2 55.2 reduce-scatter.14
  392.3 70.6 reduce-scatter.12
  466.4 67.4 reduce-scatter.8
  536.5 67.2 reduce-scatter.16
  606.4 66.9 reduce-scatter.10
  676.7 67.2 reduce-scatter.6
where the time goes:
time: 769 us; the launch traced here: 755 us
  waiting for transfers between devices  450 us (59%)
  local copies, waits for them, and re-layouts  135 us (18%)
  starting transfers between devices  88.6 us (12%)
  other arithmetic  43.8 us (6%)
  matrix products  22.8 us (3%)
  between operations  14.9 us (2%)
    reduce_scatter x1, waiting for transfers between devices, body(): lax.psum_scatter(grads[3], 'dp', scatter_dimension=1, tiled=True)  72.2 us
    reduce_scatter x1, waiting for transfers between devices, body(): lax.psum_scatter(grads[0], 'dp', scatter_dimension=1, tiled=True)  69.2 us
    reduce_scatter x1, waiting for transfers between devices, body(): lax.psum_scatter(grads[5], 'dp', scatter_dimension=1, tiled=True)  68.6 us
    reduce_scatter x1, waiting for transfers between devices, body(): lax.psum_scatter(grads[1], 'dp', scatter_dimension=1, tiled=True)  68 us
    reduce_scatter x1, waiting for transfers between devices, body(): lax.psum_scatter(grads[2], 'dp', scatter_dimension=1, tiled=True)  64.8 us
    scatter x1, local copies, waits for them, and re-layouts, body(): returning = jnp.full((lane_count,), tok_rows, jnp.int32).at[jnp.where(arr...  38.1 us
    scatter x1, local copies, waits for them, and re-layouts, body(): incoming = jnp.zeros((tok_rows,), jnp.int32).at[jnp.where(arriving, slot_...  38 us
    another operation x3, other arithmetic  26.6 us
  transfers between devices with their start and end apart: 20, of which 17 were waited for; matrix products, arithmetic and copies ran while one was open for 24% of the time, Pallas kernels for 0%

commit v1 on v0

v1 whole, which is shorter than its diff:
```python
import jax
import jax.numpy as jnp
from jax import lax
from jax.experimental import pallas as pl
from jax.experimental.pallas import tpu as pltpu
from jax.sharding import PartitionSpec as P

MESH = pl.DeviceIdType.MESH
BF = jnp.bfloat16
F32 = jnp.float32
I32 = jnp.int32

GATE1, UP1, GATE2, UP2, DOWN1, DOWN2, CT, DSG, GGRAD, UGRAD, GSG, USG = range(12)
WG, WGT, WU, WUT, WD, WDT, LG, LGT, LU, LUT, LD, LDT = range(12)


def dot_nn(a, b):
    return lax.dot_general(a, b, (((1,), (0,)), ((), ())), preferred_element_type=F32)


def dot_nt(a, b):
    return lax.dot_general(a, b, (((1,), (1,)), ((), ())), preferred_element_type=F32)


def dot_tn(a, b):
    return lax.dot_general(a, b, (((0,), (0,)), ((), ())), preferred_element_type=F32)


def tiles(total, width):
    return [(s, min(width, total - s)) for s in range(0, total, width)]


def loop(count, step):
    def run(i, carry):
        step(i)
        return carry

    lax.fori_loop(0, count, run, 0)


def at(i, width):
    return pl.ds(pl.multiple_of(i * width, width), width)


def iota(shape, dim):
    return lax.broadcasted_iota(I32, shape, dim)


def kernel(
    weights_ref, earlier_ref, dest_ref, cot_ref, rg_ref, lg_ref, ru_ref, lu_ref, rd_ref, ld_ref,
    out_ref, mgrad_ref, g0_ref, g1_ref, g2_ref, g3_ref, g4_ref, g5_ref,
    send, recv, zsend, zrecv, gsend, grecv, mats, perm1t, perm1, perm2t, perm2, tmp_a, tmp_b,
    mixed, hidden, act, slope, pick_rows, pick_slots, pick_wide, prefix, ranks, row_of, cperm,
    ssem, rsem, zssem, zrsem,
):
    n_feat, slab, slots = send.shape[1:]
    n_dp, lanes_out, width = zsend.shape[1:]
    feats, rows = cot_ref.shape
    me_f = lax.axis_index("feat")
    me_g = lax.axis_index("dp")
    cap = lanes_out // 4
    n_lanes = n_dp * cap
    main = n_dp * 32

    def feat_peer(k):
        return lax.rem(me_f + lax.rem(k * 11, n_feat), n_feat)

    def dp_peer(i):
        return lax.rem(me_g + 8 + ((i + 1) // 2) * (1 - 2 * lax.rem(i, 2)), n_dp)

    barrier = pltpu.get_barrier_semaphore()
    loop(n_feat - 1, lambda i: pl.semaphore_signal(
        barrier, inc=1, device_id={"feat": feat_peer(i + 1)}, device_id_type=MESH))
    loop(n_dp - 1, lambda i: pl.semaphore_signal(
        barrier, inc=1, device_id={"dp": dp_peer(i)}, device_id_type=MESH))

    def start_feat(n):
        def step(i):
            peer = feat_peer(i + 1)
            pltpu.make_async_remote_copy(
                src_ref=send.at[n, peer], dst_ref=recv.at[n, me_f],
                send_sem=ssem.at[n], recv_sem=rsem.at[n],
                device_id={"feat": peer}, device_id_type=MESH,
            ).start()

        loop(n_feat - 1, step)
        recv[n, me_f] = send[n, me_f]

    def feat_all(n):
        return pltpu.make_async_remote_copy(
            src_ref=send.at[n, pl.ds(0, n_feat - 1)], dst_ref=recv.at[n, pl.ds(0, n_feat - 1)],
            send_sem=ssem.at[n], recv_sem=rsem.at[n],
            device_id={"feat": feat_peer(1)}, device_id_type=MESH,
        )

    def dp_bufs(n):
        return (zsend.at[n], zrecv.at[n]) if n < 2 else (gsend.at[n - 2], grecv.at[n - 2])

    def start_dp(n):
        source, target = dp_bufs(n)

        def step(i):
            peer = dp_peer(i)
            pltpu.make_async_remote_copy(
                src_ref=source.at[peer], dst_ref=target.at[me_g],
                send_sem=zssem.at[n], recv_sem=zrsem.at[n],
                device_id={"dp": peer}, device_id_type=MESH,
            ).start()

        loop(n_dp - 1, step)
        target[me_g] = source[me_g]

    def dp_all(n):
        source, target = dp_bufs(n)
        return pltpu.make_async_remote_copy(
            src_ref=source.at[pl.ds(0, n_dp - 1)], dst_ref=target.at[pl.ds(0, n_dp - 1)],
            send_sem=zssem.at[n], recv_sem=zrsem.at[n],
            device_id={"dp": dp_peer(0)}, device_id_type=MESH,
        )

    def build_perms():
        def step(i):
            here = at(i, 128)
            r, c = iota((128, feats), 0) + i * 128, iota((128, feats), 1)
            q, a, b = r >> 4, (r >> 2) & 3, r & 3
            perm1t[here, :] = (c == a * 128 + 4 * q + b).astype(F32).astype(BF)
            perm2t[here, :] = (c == b * 128 + 4 * q + a).astype(F32).astype(BF)
            q, a, b = c >> 4, (c >> 2) & 3, c & 3
            perm1[here, :] = (r == a * 128 + 4 * q + b).astype(F32).astype(BF)
            perm2[here, :] = (r == b * 128 + 4 * q + a).astype(F32).astype(BF)

        loop(feats // 128, step)

    def square(dst, first, second, dot):
        def step(i):
            dst[at(i, 128), :] = dot(first[at(i, 128), :], second[...]).astype(BF)

        loop(feats // 128, step)

    def build_right(factor, w, wt):
        def step(i):
            w[:, at(i, 128)] = dot_nt(perm1t[:, at(i, 128)], factor[i]).astype(BF)
            wt[at(i, 128), :] = dot_nt(factor[i], perm1t[:, at(i, 128)]).astype(BF)

        loop(4, step)

    def build_left(factor, w, wt):
        def step(i):
            tmp_a[:, at(i, 128)] = dot_nn(perm2t[:, at(i, 128)], factor[i]).astype(BF)
            tmp_b[:, at(i, 128)] = dot_nt(perm2t[:, at(i, 128)], factor[i]).astype(BF)

        loop(4, step)
        square(wt, tmp_a.at[:, pl.ds(0, feats)], perm2t, dot_nt)
        square(w, tmp_b.at[:, pl.ds(0, feats)], perm2t, dot_nt)

    def flat(ref, n, s, w):
        return ref[n, :, :, pl.ds(s, w)].reshape(feats, w)

    def got(n):
        return lambda s, w: flat(recv, n, s, w)

    def plain(ref):
        return lambda s, w: ref[:, pl.ds(s, w)]

    def to_send(n):
        def put(s, w, value):
            send[n, :, :, pl.ds(s, w)] = value.astype(BF).reshape(n_feat, slab, w)

        return put

    def to_ref(ref):
        def put(s, w, value):
            ref[:, pl.ds(s, w)] = value.astype(ref.dtype)

        return put

    def product(put, mat, load, total=slots, step=256):
        for s, w in tiles(total, step):
            put(s, w, dot_nn(mat[...], load(s, w)))

    def to_lanes(n, pick, load):
        rest = []
        for c in range(4):
            value = dot_nt(pick[...], load(c))
            zsend[n, :, pl.ds(c * 32, 32), :] = value[:main].reshape(n_dp, 32, width).astype(BF)
            rest.append(value[main:].reshape(n_dp, 8, width))
        for h in range(2):
            pair = jnp.concatenate(rest[2 * h : 2 * h + 2], axis=1).astype(BF)
            zsend[n, :, pl.ds(128 + 16 * h, 16), :] = pair

    def from_lanes(n, pick, c):
        head = zrecv[n, :, pl.ds(c * 32, 32), :].reshape(main, width)
        pair = zrecv[n, :, pl.ds(128 + 16 * (c // 2), 16), :].astype(F32)
        tail = pair[:, 8 * (c % 2) : 8 * (c % 2) + 8, :].reshape(n_dp * 8, width).astype(BF)
        return dot_tn(jnp.concatenate([head, tail], axis=0), pick[...])

    def grad(n, first, second):
        parts = []
        for c in range(4):
            here = pl.ds(c * 128, 128)
            parts.append(dot_nt(first[here, :], second[here, :]).reshape(n_dp, 8, 128))
        gsend[n - 2] = jnp.concatenate(parts, axis=1).astype(BF)
        start_dp(n)

    def grad_left(n, spread, outgrad):
        product(to_ref(tmp_a), perm2, got(spread))
        product(to_ref(tmp_b), perm2, got(outgrad))
        grad(n, tmp_a, tmp_b)

    def finish_grad(n, ref):
        dp_all(n).wait_recv()
        total = jnp.sum(grecv[n - 2].astype(F32), axis=0) * ((rows * n_dp) ** (-0.5))
        ref[...] = total.reshape(4, 8, 128)

    def mix(i):
        here = at(i, 64)
        total = jnp.zeros((64, slots), F32)
        for k in range(earlier_ref.shape[0]):
            total = total + weights_ref[k] * earlier_ref[k, here, :].astype(F32)
        mixed[here, :] = total.astype(BF)

    loop(feats // 64, mix)
    build_perms()
    build_right(rg_ref, mats.at[WG], mats.at[WGT])
    build_right(ru_ref, mats.at[WU], mats.at[WUT])
    product(to_send(GATE1), mats.at[WG], plain(mixed))
    product(to_send(UP1), mats.at[WU], plain(mixed))

    def prefix_step(i):
        r, c = iota((128, slots), 0) + i * 128, iota((128, slots), 1)
        prefix[at(i, 128), :] = (r < c).astype(F32).astype(BF)

    loop(slots // 128, prefix_step)
    dest = dest_ref[...]
    inside = (dest >> 9) == me_g
    rank = dot_nn(inside.astype(F32).astype(BF), prefix[...])
    ranks[...] = jnp.where(inside, rank, -1.0)
    row_of[...] = (dest - me_g * rows).astype(F32)

    def rows_step(s):
        hit = iota((cap, slots), 0).astype(F32) == ranks[pl.ds(s, 1), :]
        row = jnp.sum(jnp.where(hit, row_of[pl.ds(s, 1), :] + 1.0, 0.0), axis=1, keepdims=True)
        chosen = (row == (iota((cap, rows), 1) + 1).astype(F32)).astype(F32)
        pick_wide[at(s, 32), :] = chosen[:32]
        pick_wide[pl.ds(pl.multiple_of(main + s * 8, 8), 8), :] = chosen[32:]

    loop(n_dp, rows_step)

    def narrow_step(i):
        pick_rows[at(i, 128), :] = pick_wide[at(i, 128), :].astype(BF)

    loop(n_lanes // 128, narrow_step)
    mine = dest_ref[pl.ds(me_g, 1), :]
    target = mine >> 9
    member = iota((n_dp, slots), 0) == target
    rank = dot_nn(member.astype(F32).astype(BF), prefix[...])
    rank = jnp.sum(jnp.where(member, rank, 0.0), axis=0, keepdims=True).astype(I32)
    lane = jnp.where(rank < 32, target * 32 + rank, main + target * 8 + rank - 32)
    lane = jnp.where(mine >= 0, lane, -1)

    def slots_step(i):
        pick_slots[at(i, 128), :] = (iota((128, slots), 0) + i * 128 == lane).astype(F32).astype(BF)

    loop(n_lanes // 128, slots_step)
    product(to_ref(cperm), perm1t, plain(cot_ref), total=rows)
    to_lanes(0, pick_rows, lambda c: cperm[pl.ds(c * 128, 128), :])

    pl.semaphore_wait(barrier, n_feat + n_dp - 2)
    start_feat(GATE1)
    start_dp(0)
    start_feat(UP1)

    build_left(lg_ref, mats.at[LG], mats.at[LGT])
    build_left(lu_ref, mats.at[LU], mats.at[LUT])
    build_left(ld_ref, mats.at[LD], mats.at[LDT])
    build_right(rd_ref, tmp_a.at[:, pl.ds(0, feats)], tmp_b.at[:, pl.ds(0, feats)])
    square(mats.at[WD], tmp_a.at[:, pl.ds(0, feats)], perm1t, dot_nt)
    square(mats.at[WDT], perm1t, tmp_b.at[:, pl.ds(0, feats)], dot_nn)

    feat_all(GATE1).wait_recv()
    product(to_send(GATE2), mats.at[LG], got(GATE1))
    start_feat(GATE2)
    feat_all(UP1).wait_recv()
    product(to_send(UP2), mats.at[LU], got(UP1))
    start_feat(UP2)

    dp_all(0).wait_recv()
    for c in range(4):
        value = from_lanes(0, pick_slots, c).astype(BF)
        send[CT, pl.ds(c * 8, 8)] = value.reshape(8, slab, slots)
    start_feat(CT)

    feat_all(GATE2).wait_recv()
    feat_all(UP2).wait_recv()

    def activate(i):
        here = at(i, 128)
        gate = recv[GATE2, :, :, here].reshape(feats, 128).astype(F32)
        up = recv[UP2, :, :, here].reshape(feats, 128).astype(F32)
        scale = 0.7978845608028654
        square_ = gate * gate
        t = jnp.tanh(scale * (gate + 0.044715 * (square_ * gate)))
        half = 0.5 * (1.0 + t)
        gelu = gate * half
        act[:, here] = gelu
        inner = scale * (1.0 + 3 * 0.044715 * square_)
        slope[:, here] = up * (half + 0.5 * gate * ((1.0 - t * t) * inner))
        hidden[:, here] = (gelu * up).astype(BF)

    loop(slots // 128, activate)
    product(to_send(DOWN1), mats.at[WD], plain(hidden))
    start_feat(DOWN1)

    feat_all(CT).wait_recv()
    product(to_send(DSG), mats.at[LDT], got(CT))
    start_feat(DSG)

    feat_all(DOWN1).wait_recv()
    product(to_send(DOWN2), mats.at[LD], got(DOWN1))
    start_feat(DOWN2)

    feat_all(DSG).wait_recv()
    for s, w in tiles(slots, 128):
        hidden_grad = dot_nn(mats[WDT], flat(recv, DSG, s, w))
        to_send(GGRAD)(s, w, hidden_grad * slope[:, pl.ds(s, w)])
        to_send(UGRAD)(s, w, hidden_grad * act[:, pl.ds(s, w)])
    start_feat(GGRAD)
    start_feat(UGRAD)

    grad_left(7, DOWN1, CT)
    product(to_ref(tmp_a), perm1, plain(hidden))
    product(to_ref(tmp_b), perm1, got(DSG))
    grad(6, tmp_a, tmp_b)

    feat_all(GGRAD).wait_recv()
    product(to_send(GSG), mats.at[LGT], got(GGRAD))
    start_feat(GSG)
    feat_all(UGRAD).wait_recv()
    product(to_send(USG), mats.at[LUT], got(UGRAD))
    start_feat(USG)

    feat_all(DOWN2).wait_recv()
    to_lanes(1, pick_slots, lambda c: recv[DOWN2, pl.ds(c * 8, 8)].reshape(128, slots))
    start_dp(1)

    grad_left(3, GATE1, GGRAD)
    grad_left(5, UP1, UGRAD)

    feat_all(GSG).wait_recv()
    product(to_ref(tmp_b), perm1, got(GSG))
    grad(2, mixed, tmp_b)
    feat_all(USG).wait_recv()
    product(to_ref(tmp_b), perm1, got(USG))
    grad(4, mixed, tmp_b)
    for s, w in tiles(slots, 256):
        value = dot_nn(mats[WGT], flat(recv, GSG, s, w)) + dot_nn(mats[WUT], flat(recv, USG, s, w))
        mgrad_ref[:, pl.ds(s, w)] = value.astype(BF)

    dp_all(1).wait_recv()
    for c in range(4):
        cperm[pl.ds(c * 128, 128), :] = from_lanes(1, pick_rows, c).astype(BF)
    product(to_ref(out_ref), perm1, plain(cperm), total=rows)

    finish_grad(6, g4_ref)
    finish_grad(7, g5_ref)
    finish_grad(3, g1_ref)
    finish_grad(5, g3_ref)
    finish_grad(2, g0_ref)
    finish_grad(4, g2_ref)
    for n in range(12):
        feat_all(n).wait_send()
    for n in range(8):
        dp_all(n).wait_send()


def body(earlier, mix_weights, destinations, cotangent, *factors):
    n_feat, n_dp = lax.axis_size("feat"), lax.axis_size("dp")
    feats, slots = earlier.shape[1:]
    rows = cotangent.shape[1]
    slab = feats // n_feat
    cap = slots // n_dp
    grad_shape = (factors[0].shape[0], factors[0].shape[1] // n_dp, factors[0].shape[2])
    vmem = pl.BlockSpec(memory_space=pltpu.VMEM)
    wide = pltpu.VMEM((feats, slots), BF)
    square = pltpu.VMEM((feats, feats), BF)
    return pl.pallas_call(
        kernel,
        out_shape=(
            jax.ShapeDtypeStruct((feats, rows), BF),
            jax.ShapeDtypeStruct((feats, slots), BF),
        )
        + (jax.ShapeDtypeStruct(grad_shape, F32),) * 6,
        in_specs=[pl.BlockSpec(memory_space=pltpu.SMEM)] + [vmem] * 9,
        out_specs=(vmem,) * 8,
        scratch_shapes=[
            pltpu.VMEM((12, n_feat, slab, slots), BF),
            pltpu.VMEM((12, n_feat, slab, slots), BF),
            pltpu.VMEM((2, n_dp, 4 * cap, 128), BF),
            pltpu.VMEM((2, n_dp, 4 * cap, 128), BF),
            pltpu.VMEM((6, n_dp, 32, 128), BF),
            pltpu.VMEM((6, n_dp, 32, 128), BF),
            pltpu.VMEM((12, feats, feats), BF),
            square, square, square, square,
            wide, wide, wide, wide,
            pltpu.VMEM((feats, slots), F32),
            pltpu.VMEM((feats, slots), F32),
            pltpu.VMEM((n_dp * cap, rows), BF),
            pltpu.VMEM((n_dp * cap, slots), BF),
            pltpu.VMEM((n_dp * cap, rows), F32),
            pltpu.VMEM((slots, slots), BF),
            pltpu.VMEM((n_dp, slots), F32),
            pltpu.VMEM((n_dp, slots), F32),
            pltpu.VMEM((feats, rows), BF),
            pltpu.SemaphoreType.DMA((12,)),
            pltpu.SemaphoreType.DMA((12,)),
            pltpu.SemaphoreType.DMA((8,)),
            pltpu.SemaphoreType.DMA((8,)),
        ],
        compiler_params=pltpu.CompilerParams(
            collective_id=0, has_side_effects=True, vmem_limit_bytes=60 << 20
        ),
    )(mix_weights, earlier, destinations.reshape(n_dp, slots), cotangent, *factors)


def solution(mesh):
    factor, grad = P("feat", None, None), P("feat", "dp", None)
    return jax.shard_map(
        body,
        mesh=mesh,
        in_specs=(P(None, "feat", "dp"), P(), P(), P("feat", "dp")) + (factor,) * 6,
        out_specs=(P("feat", "dp"), P("feat", "dp")) + (grad,) * 6,
        check_vma=False,
    )
```

time: 769 us -> 167 us (0.22); the launches traced: 755 us -> 167 us
  waiting for transfers between devices: 450 us -> 0 us
  Pallas kernels: 0 us -> 157 us
  local copies, waits for them, and re-layouts: 135 us -> 8.94 us
  starting transfers between devices: 88.6 us -> 0 us
  other arithmetic: 43.8 us -> 0 us
  matrix products: 22.8 us -> 0 us
  between operations: 14.9 us -> 0.7 us
    reduce_scatter x6 -> x0, waiting for transfers between devices: 345 us -> none  [the longest x1 72.2 us: body(): lax.psum_scatter(grads[3], 'dp', scatter_dimension=1, tiled=True)]
    pallas_call x0 -> x1, Pallas kernels: none -> 157 us  [body(): pl.pallas_call(kernel, out_shape=(jax.ShapeDtypeStruct((feats, rows), BF)...]
    all_to_all x14 -> x0, waiting for transfers between devices: 105 us -> none  [the longest x2 25.4 us: body(): lax.all_to_all(lane_data, 'dp', split_axis=1, concat_axis=1, tiled=True)]
    all_to_all x14 -> x0, starting transfers between devices: 88.3 us -> none  [the longest x2 19.3 us: body(): lax.all_to_all(lane_data, 'dp', split_axis=1, concat_axis=1, tiled=True)]
    scatter x3 -> x0, local copies, waits for them, and re-layouts: 80.2 us -> none  [the longest x1 38.1 us: body(): returning = jnp.full((lane_count,), tok_rows, jnp.int32).at[jnp.where(arr...]
    another operation x3 -> x0, other arithmetic: 26.6 us -> none
    dot_general x18 -> x0, matrix products: 22.8 us -> none  [the longest x3 5.41 us: left_grad(): jnp.einsum('iot,pot->oip', spread, out_grad, preferred_element_type=jnp.f...]
    convert_element_type x15 -> x0, local copies, waits for them, and re-layouts: 20.1 us -> none  [the longest x3 4.86 us: right_apply(): return jnp.einsum('ijt,ijo->iot', values, right_factor, preferred_element...]
  transfers between devices with their start and end apart: 20 -> 0, of which waited for: 17 -> 0; matrix products, arithmetic and copies ran while one was open for 24% -> 0% of each run, Pallas kernels for 0% -> 0%
where the time goes in v1:
time: 167 us
  Pallas kernels  157 us (94%)
  local copies, waits for them, and re-layouts  8.94 us (5%)
    pallas_call x1, Pallas kernels, body(): pl.pallas_call(kernel, out_shape=(jax.ShapeDtypeStruct((feats, rows), BF)...  157 us
    unnamed x20, local copies, waits for them, and re-layouts  7.54 us

profile of v1, /device:TPU:1, one launch (start us, length us, event | category | flops | bytes accessed | tf_op | source)
XLA Modules:
  0.0 167.0 jit_solution(7468936459616304329)
XLA Ops:
  0.6 1.4 reshape.19.dest_ref
  2.0 157.4 %shard_map.161 = (bf16[512,512]{1,0:T(8,128)(2,1)}, bf16[512,640]{1,0:T(8,128)(2,1)}, f32[4,8,128]{2,1,0:T(8,128)}, f32[4,8,128]{2,1,0:T(8,128)}, f32[4,8,128]{2...) custom-call(f32[3]{0:T(128)} %weights_ref.1, bf16[3,512,640]{2,1,0:T(8,128)(2,1)} %earlier_ref.1, ...), custom_call_target="tpu_custom_call" | custom-call | tf_op jit(solution)/shard_map/pallas_call | solution.py:386
  159.5 0.0 copy-start.5
  159.5 0.0 copy-start.4
  159.5 0.0 copy-start.3
  159.5 0.0 copy-start.2
  159.5 0.0 copy-start.1
  159.5 0.0 copy-start
  159.5 1.9 %copy.26 = bf16[512,512]{1,0:T(8,128)(2,1)} copy(bf16[512,512]{1,0:T(8,128)(2,1)} %get-tuple-element.16) | data formatting | bytes 1048576
  161.4 2.0 %copy.27 = bf16[512,640]{1,0:T(8,128)(2,1)} copy(bf16[512,640]{1,0:T(8,128)(2,1)} %get-tuple-element.17) | data formatting | bytes 1310720
  163.4 0.0 copy-done.5
  163.4 0.6 copy.28
  164.0 0.0 copy-done.4
  164.0 0.6 copy.29
  164.6 0.0 copy-done.3
  164.6 0.6 copy.30
  165.2 0.0 copy-done.2
  165.2 0.6 copy.31
  165.8 0.0 copy-done.1
  165.8 0.6 copy.32
  166.4 0.0 copy-done
  166.4 0.6 copy.33
Async XLA Ops:
  159.5 3.9 %copy-start.5 = (f32[4,8,128]{2,1,0:T(8,128)S(1)}, f32[4,8,128]{2,1,0:T(8,128)}, u32[]{:S(2)}) copy-start(f32[4,8,128]{2,1,0:T(8,128)} %get-tuple-element.18) | copy-start | bytes 49156
  159.5 4.5 %copy-start.4 = (f32[4,8,128]{2,1,0:T(8,128)S(1)}, f32[4,8,128]{2,1,0:T(8,128)}, u32[]{:S(2)}) copy-start(f32[4,8,128]{2,1,0:T(8,128)} %get-tuple-element.19) | copy-start | bytes 49156
  159.5 5.1 %copy-start.3 = (f32[4,8,128]{2,1,0:T(8,128)S(1)}, f32[4,8,128]{2,1,0:T(8,128)}, u32[]{:S(2)}) copy-start(f32[4,8,128]{2,1,0:T(8,128)} %get-tuple-element.20) | copy-start | bytes 49156
  159.5 5.7 %copy-start.2 = (f32[4,8,128]{2,1,0:T(8,128)S(1)}, f32[4,8,128]{2,1,0:T(8,128)}, u32[]{:S(2)}) copy-start(f32[4,8,128]{2,1,0:T(8,128)} %get-tuple-element.21) | copy-start | bytes 49156
  159.5 6.3 %copy-start.1 = (f32[4,8,128]{2,1,0:T(8,128)S(1)}, f32[4,8,128]{2,1,0:T(8,128)}, u32[]{:S(2)}) copy-start(f32[4,8,128]{2,1,0:T(8,128)} %get-tuple-element.22) | copy-start | bytes 49156
  159.5 6.9 %copy-start = (f32[4,8,128]{2,1,0:T(8,128)S(1)}, f32[4,8,128]{2,1,0:T(8,128)}, u32[]{:S(2)}) copy-start(f32[4,8,128]{2,1,0:T(8,128)} %get-tuple-element.23) | copy-start | bytes 49156

commit v2 on v1

--- a/solution.py
+++ b/solution.py
@@ -47,15 +47,16 @@
 
 
 def kernel(
-    weights_ref, earlier_ref, dest_ref, cot_ref, rg_ref, lg_ref, ru_ref, lu_ref, rd_ref, ld_ref,
-    out_ref, mgrad_ref, g0_ref, g1_ref, g2_ref, g3_ref, g4_ref, g5_ref,
-    send, recv, zsend, zrecv, gsend, grecv, mats, perm1t, perm1, perm2t, perm2, tmp_a, tmp_b,
+    weights_ref, earlier_in, dest_in, cot_in, rg_in, lg_in, ru_in, lu_in, rd_in, ld_in,
+    out_ref, mgrad_ref, grads_ref,
+    earlier_ref, dest_ref, cot_ref, factors, isem,
+    send, recv, zsend, zrecv, gsend, gnear, gsum, gfar, dest_all, mats, perm1t, perm1, perm2t, perm2, tmp_a, tmp_b,
     mixed, hidden, act, slope, pick_rows, pick_slots, pick_wide, prefix, ranks, row_of, cperm,
-    ssem, rsem, zssem, zrsem,
+    ssem, rsem, zssem, zrsem, nssem, nrsem, fssem, frsem,
 ):
     n_feat, slab, slots = send.shape[1:]
     n_dp, lanes_out, width = zsend.shape[1:]
-    feats, rows = cot_ref.shape
+    feats, rows = cot_in.shape
     me_f = lax.axis_index("feat")
     me_g = lax.axis_index("dp")
     cap = lanes_out // 4
@@ -68,6 +69,16 @@
     def dp_peer(i):
         return lax.rem(me_g + 8 + ((i + 1) // 2) * (1 - 2 * lax.rem(i, 2)), n_dp)
 
+    rg_ref, lg_ref, ru_ref, lu_ref, rd_ref, ld_ref = (factors.at[n] for n in range(6))
+    loads = [
+        pltpu.make_async_copy(source, target, isem.at[n])
+        for n, (source, target) in enumerate((
+            (earlier_in, earlier_ref), (rg_in, rg_ref), (ru_in, ru_ref), (dest_in, dest_ref),
+            (cot_in, cot_ref), (lg_in, lg_ref), (lu_in, lu_ref), (rd_in, rd_ref), (ld_in, ld_ref),
+        ))
+    ]
+    for load in loads:
+        load.start()
     barrier = pltpu.get_barrier_semaphore()
     loop(n_feat - 1, lambda i: pl.semaphore_signal(
         barrier, inc=1, device_id={"feat": feat_peer(i + 1)}, device_id_type=MESH))
@@ -93,30 +104,52 @@
             device_id={"feat": feat_peer(1)}, device_id_type=MESH,
         )
 
-    def dp_bufs(n):
-        return (zsend.at[n], zrecv.at[n]) if n < 2 else (gsend.at[n - 2], grecv.at[n - 2])
-
     def start_dp(n):
-        source, target = dp_bufs(n)
-
         def step(i):
             peer = dp_peer(i)
             pltpu.make_async_remote_copy(
-                src_ref=source.at[peer], dst_ref=target.at[me_g],
+                src_ref=zsend.at[n, peer], dst_ref=zrecv.at[n, me_g],
                 send_sem=zssem.at[n], recv_sem=zrsem.at[n],
                 device_id={"dp": peer}, device_id_type=MESH,
             ).start()
 
         loop(n_dp - 1, step)
-        target[me_g] = source[me_g]
+        zrecv[n, me_g] = zsend[n, me_g]
 
     def dp_all(n):
-        source, target = dp_bufs(n)
         return pltpu.make_async_remote_copy(
-            src_ref=source.at[pl.ds(0, n_dp - 1)], dst_ref=target.at[pl.ds(0, n_dp - 1)],
+            src_ref=zsend.at[n, pl.ds(0, n_dp - 1)], dst_ref=zrecv.at[n, pl.ds(0, n_dp - 1)],
             send_sem=zssem.at[n], recv_sem=zrsem.at[n],
             device_id={"dp": dp_peer(0)}, device_id_type=MESH,
         )
+
+    def near(n, h):
+        return pltpu.make_async_remote_copy(
+            src_ref=gsend.at[n, pl.ds(12 * h, 5)], dst_ref=gnear.at[n, h],
+            send_sem=nssem.at[n, h], recv_sem=nrsem.at[n, h],
+            device_id={"dp": lax.rem(me_g + (1, n_dp - 1)[h], n_dp)}, device_id_type=MESH,
+        )
+
+    def far(n, j):
+        return pltpu.make_async_remote_copy(
+            src_ref=gsum.at[n, j], dst_ref=gfar.at[n, j],
+            send_sem=fssem.at[n], recv_sem=frsem.at[n],
+            device_id={"dp": lax.rem(me_g + 2 * n_dp - 2 - 3 * j, n_dp)}, device_id_type=MESH,
+        )
+
+    def far_all(n):
+        return pltpu.make_async_remote_copy(
+            src_ref=gsum.at[n], dst_ref=gfar.at[n], send_sem=fssem.at[n], recv_sem=frsem.at[n],
+            device_id={"dp": lax.rem(me_g + 1, n_dp)}, device_id_type=MESH,
+        )
+
+    def relay(n):
+        near(n, 0).wait_recv()
+        near(n, 1).wait_recv()
+        total = gsend[n, pl.ds(6, 5)].astype(F32) + gnear[n, 0].astype(F32) + gnear[n, 1].astype(F32)
+        gsum[n] = total.astype(BF)
+        for j in range(5):
+            far(n, j).start()
 
     def build_perms():
         def step(i):
@@ -131,27 +164,35 @@
 
         loop(feats // 128, step)
 
-    def square(dst, first, second, dot):
-        def step(i):
-            dst[at(i, 128), :] = dot(first[at(i, 128), :], second[...]).astype(BF)
-
-        loop(feats // 128, step)
-
-    def build_right(factor, w, wt):
+    def square(dst, first, second):
+        for s, w in tiles(feats, 256):
+            dst[:, pl.ds(s, w)] = dot_nn(first[...], second[:, pl.ds(s, w)]).astype(BF)
+
+    def build_right(factor, w):
         def step(i):
             w[:, at(i, 128)] = dot_nt(perm1t[:, at(i, 128)], factor[i]).astype(BF)
+
+        loop(4, step)
+
+    def build_right_back(factor, wt):
+        def step(i):
             wt[at(i, 128), :] = dot_nt(factor[i], perm1t[:, at(i, 128)]).astype(BF)
 
         loop(4, step)
 
-    def build_left(factor, w, wt):
+    def build_left(factor, w):
+        def step(i):
+            tmp_b[:, at(i, 128)] = dot_nt(perm2t[:, at(i, 128)], factor[i]).astype(BF)
+
+        loop(4, step)
+        square(w, tmp_b.at[:, pl.ds(0, feats)], perm2)
+
+    def build_left_back(factor, wt):
         def step(i):
             tmp_a[:, at(i, 128)] = dot_nn(perm2t[:, at(i, 128)], factor[i]).astype(BF)
-            tmp_b[:, at(i, 128)] = dot_nt(perm2t[:, at(i, 128)], factor[i]).astype(BF)
 
         loop(4, step)
-        square(wt, tmp_a.at[:, pl.ds(0, feats)], perm2t, dot_nt)
-        square(w, tmp_b.at[:, pl.ds(0, feats)], perm2t, dot_nt)
+        square(wt, tmp_a.at[:, pl.ds(0, feats)], perm2)
 
     def flat(ref, n, s, w):
         return ref[n, :, :, pl.ds(s, w)].reshape(feats, w)
@@ -199,18 +240,22 @@
         for c in range(4):
             here = pl.ds(c * 128, 128)
             parts.append(dot_nt(first[here, :], second[here, :]).reshape(n_dp, 8, 128))
-        gsend[n - 2] = jnp.concatenate(parts, axis=1).astype(BF)
-        start_dp(n)
+        packed = jnp.concatenate(parts, axis=1).astype(BF)
+        for g in range(n_dp):
+            m = lax.rem(me_g + 2 * n_dp - 1 - g, n_dp)
+            gsend[n, lax.rem(m, 3) * 6 + m // 3] = packed[g]
+        near(n, 0).start()
+        near(n, 1).start()
 
     def grad_left(n, spread, outgrad):
         product(to_ref(tmp_a), perm2, got(spread))
         product(to_ref(tmp_b), perm2, got(outgrad))
         grad(n, tmp_a, tmp_b)
 
-    def finish_grad(n, ref):
-        dp_all(n).wait_recv()
-        total = jnp.sum(grecv[n - 2].astype(F32), axis=0) * ((rows * n_dp) ** (-0.5))
-        ref[...] = total.reshape(4, 8, 128)
+    def finish_grad(n):
+        far_all(n).wait_recv()
+        total = gsend[n, 5].astype(F32) + jnp.sum(gfar[n].astype(F32), axis=0)
+        grads_ref[n] = total * ((rows * n_dp) ** (-0.5))
 
     def mix(i):
         here = at(i, 64)
@@ -219,11 +264,14 @@
             total = total + weights_ref[k] * earlier_ref[k, here, :].astype(F32)
         mixed[here, :] = total.astype(BF)
 
+    build_perms()
+    loads[0].wait()
     loop(feats // 64, mix)
-    build_perms()
-    build_right(rg_ref, mats.at[WG], mats.at[WGT])
-    build_right(ru_ref, mats.at[WU], mats.at[WUT])
+    loads[1].wait()
+    build_right(rg_ref, mats.at[WG])
     product(to_send(GATE1), mats.at[WG], plain(mixed))
+    loads[2].wait()
+    build_right(ru_ref, mats.at[WU])
     product(to_send(UP1), mats.at[WU], plain(mixed))
 
     def prefix_step(i):
@@ -231,7 +279,10 @@
         prefix[at(i, 128), :] = (r < c).astype(F32).astype(BF)
 
     loop(slots // 128, prefix_step)
-    dest = dest_ref[...]
+    loads[3].wait()
+    for b in range(slots // 128):
+        dest_all[:, pl.ds(b * 128, 128)] = dest_ref[pl.ds(b, n_dp, stride=slots // 128), :]
+    dest = dest_all[...]
     inside = (dest >> 9) == me_g
     rank = dot_nn(inside.astype(F32).astype(BF), prefix[...])
     ranks[...] = jnp.where(inside, rank, -1.0)
@@ -241,16 +292,25 @@
         hit = iota((cap, slots), 0).astype(F32) == ranks[pl.ds(s, 1), :]
         row = jnp.sum(jnp.where(hit, row_of[pl.ds(s, 1), :] + 1.0, 0.0), axis=1, keepdims=True)
         chosen = (row == (iota((cap, rows), 1) + 1).astype(F32)).astype(F32)
-        pick_wide[at(s, 32), :] = chosen[:32]
-        pick_wide[pl.ds(pl.multiple_of(main + s * 8, 8), 8), :] = chosen[32:]
-
-    loop(n_dp, rows_step)
+        pick_wide[pl.ds(s * 32, 32), :] = chosen[:32]
+        pick_wide[pl.ds(main + s * 8, 8), :] = chosen[32:]
+
+    for s in range(n_dp):
+        rows_step(s)
 
     def narrow_step(i):
         pick_rows[at(i, 128), :] = pick_wide[at(i, 128), :].astype(BF)
 
     loop(n_lanes // 128, narrow_step)
-    mine = dest_ref[pl.ds(me_g, 1), :]
+    loads[4].wait()
+    product(to_ref(cperm), perm1t, plain(cot_ref), total=rows)
+    to_lanes(0, pick_rows, lambda c: cperm[pl.ds(c * 128, 128), :])
+    pl.semaphore_wait(barrier, n_feat + n_dp - 2)
+    start_dp(0)
+    start_feat(GATE1)
+    start_feat(UP1)
+
+    mine = dest_all[pl.ds(me_g, 1), :]
     target = mine >> 9
     member = iota((n_dp, slots), 0) == target
     rank = dot_nn(member.astype(F32).astype(BF), prefix[...])
@@ -262,20 +322,10 @@
         pick_slots[at(i, 128), :] = (iota((128, slots), 0) + i * 128 == lane).astype(F32).astype(BF)
 
     loop(n_lanes // 128, slots_step)
-    product(to_ref(cperm), perm1t, plain(cot_ref), total=rows)
-    to_lanes(0, pick_rows, lambda c: cperm[pl.ds(c * 128, 128), :])
-
-    pl.semaphore_wait(barrier, n_feat + n_dp - 2)
-    start_feat(GATE1)
-    start_dp(0)
-    start_feat(UP1)
-
-    build_left(lg_ref, mats.at[LG], mats.at[LGT])
-    build_left(lu_ref, mats.at[LU], mats.at[LUT])
-    build_left(ld_ref, mats.at[LD], mats.at[LDT])
-    build_right(rd_ref, tmp_a.at[:, pl.ds(0, feats)], tmp_b.at[:, pl.ds(0, feats)])
-    square(mats.at[WD], tmp_a.at[:, pl.ds(0, feats)], perm1t, dot_nt)
-    square(mats.at[WDT], perm1t, tmp_b.at[:, pl.ds(0, feats)], dot_nn)
+    loads[5].wait()
+    build_left(lg_ref, mats.at[LG])
+    loads[6].wait()
+    build_left(lu_ref, mats.at[LU])
 
     feat_all(GATE1).wait_recv()
     product(to_send(GATE2), mats.at[LG], got(GATE1))
@@ -283,6 +333,19 @@
     feat_all(UP1).wait_recv()
     product(to_send(UP2), mats.at[LU], got(UP1))
     start_feat(UP2)
+
+    loads[7].wait()
+    loads[8].wait()
+    build_right(rd_ref, tmp_a)
+    square(mats.at[WD], tmp_a.at[:, pl.ds(0, feats)], perm1)
+    build_left(ld_ref, mats.at[LD])
+    build_left_back(ld_ref, mats.at[LDT])
+    build_right_back(rd_ref, tmp_b.at[:, pl.ds(0, feats)])
+    square(mats.at[WDT], perm1t, tmp_b)
+    build_left_back(lg_ref, mats.at[LGT])
+    build_left_back(lu_ref, mats.at[LUT])
+    build_right_back(rg_ref, mats.at[WGT])
+    build_right_back(ru_ref, mats.at[WUT])
 
     dp_all(0).wait_recv()
     for c in range(4):
@@ -318,6 +381,7 @@
     feat_all(DOWN1).wait_recv()
     product(to_send(DOWN2), mats.at[LD], got(DOWN1))
     start_feat(DOWN2)
+    grad_left(5, DOWN1, CT)
 
     feat_all(DSG).wait_recv()
     for s, w in tiles(slots, 128):
@@ -327,10 +391,15 @@
     start_feat(GGRAD)
     start_feat(UGRAD)
 
-    grad_left(7, DOWN1, CT)
+
     product(to_ref(tmp_a), perm1, plain(hidden))
     product(to_ref(tmp_b), perm1, got(DSG))
-    grad(6, tmp_a, tmp_b)
+    grad(4, tmp_a, tmp_b)
+    feat_all(DOWN2).wait_recv()
+    to_lanes(1, pick_slots, lambda c: recv[DOWN2, pl.ds(c * 8, 8)].reshape(128, slots))
+    relay(5)
+    relay(4)
+    start_dp(1)
 
     feat_all(GGRAD).wait_recv()
     product(to_send(GSG), mats.at[LGT], got(GGRAD))
@@ -338,39 +407,45 @@
     feat_all(UGRAD).wait_recv()
     product(to_send(USG), mats.at[LUT], got(UGRAD))
     start_feat(USG)
-
-    feat_all(DOWN2).wait_recv()
-    to_lanes(1, pick_slots, lambda c: recv[DOWN2, pl.ds(c * 8, 8)].reshape(128, slots))
-    start_dp(1)
-
-    grad_left(3, GATE1, GGRAD)
-    grad_left(5, UP1, UGRAD)
+    grad_left(1, GATE1, GGRAD)
+    grad_left(3, UP1, UGRAD)
 
     feat_all(GSG).wait_recv()
     product(to_ref(tmp_b), perm1, got(GSG))
-    grad(2, mixed, tmp_b)
+    grad(0, mixed, tmp_b)
     feat_all(USG).wait_recv()
     product(to_ref(tmp_b), perm1, got(USG))
-    grad(4, mixed, tmp_b)
+    grad(2, mixed, tmp_b)
+    relay(1)
+    relay(3)
+    relay(0)
     for s, w in tiles(slots, 256):
         value = dot_nn(mats[WGT], flat(recv, GSG, s, w)) + dot_nn(mats[WUT], flat(recv, USG, s, w))
         mgrad_ref[:, pl.ds(s, w)] = value.astype(BF)
+    relay(2)
 
     dp_all(1).wait_recv()
     for c in range(4):
         cperm[pl.ds(c * 128, 128), :] = from_lanes(1, pick_rows, c).astype(BF)
     product(to_ref(out_ref), perm1, plain(cperm), total=rows)
 
-    finish_grad(6, g4_ref)
-    finish_grad(7, g5_ref)
-    finish_grad(3, g1_ref)
-    finish_grad(5, g3_ref)
-    finish_grad(2, g0_ref)
-    finish_grad(4, g2_ref)
+    for n in (5, 4, 1, 3, 0, 2):
+        finish_grad(n)
     for n in range(12):
         feat_all(n).wait_send()
-    for n in range(8):
+    for n in range(2):
         dp_all(n).wait_send()
+    for n in range(6):
+        near(n, 0).wait_send()
+        near(n, 1).wait_send()
+        far_all(n).wait_send()
+
+
+def hand_over(out_ref, mgrad_ref, grads_ref, out_to, mgrad_to, *grads_to):
+    out_to[...] = out_ref[...]
+    mgrad_to[...] = mgrad_ref[...]
+    for n, ref in enumerate(grads_to):
+        ref[...] = grads_ref[n].reshape(ref.shape)
 
 
 def body(earlier, mix_weights, destinations, cotangent, *factors):
@@ -383,22 +458,30 @@
     vmem = pl.BlockSpec(memory_space=pltpu.VMEM)
     wide = pltpu.VMEM((feats, slots), BF)
     square = pltpu.VMEM((feats, feats), BF)
-    return pl.pallas_call(
+    packed = (
+        jax.ShapeDtypeStruct((feats, rows), BF),
+        jax.ShapeDtypeStruct((feats, slots), BF),
+    )
+    results = pl.pallas_call(
         kernel,
-        out_shape=(
-            jax.ShapeDtypeStruct((feats, rows), BF),
-            jax.ShapeDtypeStruct((feats, slots), BF),
-        )
-        + (jax.ShapeDtypeStruct(grad_shape, F32),) * 6,
-        in_specs=[pl.BlockSpec(memory_space=pltpu.SMEM)] + [vmem] * 9,
-        out_specs=(vmem,) * 8,
+        out_shape=packed + (jax.ShapeDtypeStruct((6, 32, 128), F32),),
+        in_specs=[pl.BlockSpec(memory_space=pltpu.SMEM)] + [pl.BlockSpec(memory_space=pl.ANY)] * 9,
+        out_specs=(vmem,) * 3,
         scratch_shapes=[
+            pltpu.VMEM(earlier.shape, BF),
+            pltpu.VMEM((destinations.size // 128, 128), I32),
+            pltpu.VMEM((feats, rows), BF),
+            pltpu.VMEM((6,) + factors[0].shape, BF),
+            pltpu.SemaphoreType.DMA((9,)),
             pltpu.VMEM((12, n_feat, slab, slots), BF),
             pltpu.VMEM((12, n_feat, slab, slots), BF),
             pltpu.VMEM((2, n_dp, 4 * cap, 128), BF),
             pltpu.VMEM((2, n_dp, 4 * cap, 128), BF),
-            pltpu.VMEM((6, n_dp, 32, 128), BF),
-            pltpu.VMEM((6, n_dp, 32, 128), BF),
+            pltpu.VMEM((6, 18, 32, 128), BF),
+            pltpu.VMEM((6, 2, 5, 32, 128), BF),
+            pltpu.VMEM((6, 5, 32, 128), BF),
+            pltpu.VMEM((6, 5, 32, 128), BF),
+            pltpu.VMEM((n_dp, slots), I32),
             pltpu.VMEM((12, feats, feats), BF),
             square, square, square, square,
             wide, wide, wide, wide,
@@ -413,13 +496,23 @@
             pltpu.VMEM((feats, rows), BF),
             pltpu.SemaphoreType.DMA((12,)),
             pltpu.SemaphoreType.DMA((12,)),
-            pltpu.SemaphoreType.DMA((8,)),
-            pltpu.SemaphoreType.DMA((8,)),
+            pltpu.SemaphoreType.DMA((2,)),
+            pltpu.SemaphoreType.DMA((2,)),
+            pltpu.SemaphoreType.DMA((6, 2)),
+            pltpu.SemaphoreType.DMA((6, 2)),
+            pltpu.SemaphoreType.DMA((6,)),
+            pltpu.SemaphoreType.DMA((6,)),
         ],
         compiler_params=pltpu.CompilerParams(
             collective_id=0, has_side_effects=True, vmem_limit_bytes=60 << 20
         ),
-    )(mix_weights, earlier, destinations.reshape(n_dp, slots), cotangent, *factors)
+    )(mix_weights, earlier, destinations.reshape(-1, 128), cotangent, *factors)
+    return pl.pallas_call(
+        hand_over,
+        out_shape=packed + (jax.ShapeDtypeStruct(grad_shape, F32),) * 6,
+        in_specs=[vmem] * 3,
+        out_specs=(vmem,) * 8,
+    )(*results)
 
 
 def solution(mesh):

time: 167 us -> 136 us (0.81)
  Pallas kernels: 157 us -> 135 us
  local copies, waits for them, and re-layouts: 8.94 us -> 0 us
    pallas_call x1 -> x2, Pallas kernels: 157 us -> 135 us  [the longest x1 133 us: body(): pl.pallas_call(kernel, out_shape=packed + (jax.ShapeDtypeStruct((6, 32, 1...]
    unnamed x20 -> x0, local copies, waits for them, and re-layouts: 7.54 us -> none
where the time goes in v2:
time: 136 us
  Pallas kernels  135 us (99%)
    pallas_call x1, Pallas kernels, body(): pl.pallas_call(kernel, out_shape=packed + (jax.ShapeDtypeStruct((6, 32, 1...  133 us

profile of v2, /device:TPU:1, one launch (start us, length us, event | category | flops | bytes accessed | tf_op | source)
XLA Modules:
  0.0 136.0 jit_solution(8390018307899317102)
XLA Ops:
  0.6 133.0 %shard_map.161 = (bf16[512,512]{1,0:T(8,128)(2,1)}, bf16[512,640]{1,0:T(8,128)(2,1)}, f32[6,32,128]{2,1,0:T(8,128)}) custom-call(f32[3]{0:T(128)} %weights_ref.1, bf16[3,512,640]{2,1,0:T(8,128)(2,1)} %earlier_in.1, s32[80,128]{1,0:T(8,128)} %bitcast.1, bf16[512,512]{1,0:T(8,128)(2,1)} %cot_in.1, bf16[4,128,128]{2,1,0:T(8,128)(2,1)} %rg_in.1, ...), custom_call_target="tpu_custom_call" | custom-call | tf_op jit(solution)/shard_map/pallas_call | solution.py:465
  133.7 2.3 %shard_map.162 = (bf16[512,512]{1,0:T(8,128)(2,1)}, bf16[512,640]{1,0:T(8,128)(2,1)}, f32[4,8,128]{2,1,0:T(8,128)}, f32[4,8,128]{2,1,0:T(8,128)}, f32[4,8,128]{2...) custom-call(bf16[512,512]{1,0:T(8,128)(2,1)} %get-tuple-element.11.out_ref, ...), custom_call_target="tpu_custom_call" | custom-call | tf_op jit(solution)/shard_map/pallas_call | solution.py:510

commit v3 on v2

--- a/solution.py
+++ b/solution.py
@@ -50,9 +50,9 @@
     weights_ref, earlier_in, dest_in, cot_in, rg_in, lg_in, ru_in, lu_in, rd_in, ld_in,
     out_ref, mgrad_ref, grads_ref,
     earlier_ref, dest_ref, cot_ref, factors, isem,
-    send, recv, zsend, zrecv, gsend, gnear, gsum, gfar, dest_all, mats, perm1t, perm1, perm2t, perm2, tmp_a, tmp_b,
+    send, recv, zsend, zrecv, gsend, gnear, gsum, gfar, gall, gland, dest_all, mats, perm1t, perm1, perm2t, perm2, tmp_a, tmp_b,
     mixed, hidden, act, slope, pick_rows, pick_slots, pick_wide, prefix, ranks, row_of, cperm,
-    ssem, rsem, zssem, zrsem, nssem, nrsem, fssem, frsem,
+    ssem, rsem, zssem, zrsem, nssem, nrsem, fssem, frsem, dssem, drsem,
 ):
     n_feat, slab, slots = send.shape[1:]
     n_dp, lanes_out, width = zsend.shape[1:]
@@ -235,12 +235,15 @@
         tail = pair[:, 8 * (c % 2) : 8 * (c % 2) + 8, :].reshape(n_dp * 8, width).astype(BF)
         return dot_tn(jnp.concatenate([head, tail], axis=0), pick[...])
 
-    def grad(n, first, second):
+    def shares(first, second):
         parts = []
         for c in range(4):
             here = pl.ds(c * 128, 128)
             parts.append(dot_nt(first[here, :], second[here, :]).reshape(n_dp, 8, 128))
-        packed = jnp.concatenate(parts, axis=1).astype(BF)
+        return jnp.concatenate(parts, axis=1).astype(BF)
+
+    def grad(n, first, second):
+        packed = shares(first, second)
         for g in range(n_dp):
             m = lax.rem(me_g + 2 * n_dp - 1 - g, n_dp)
             gsend[n, lax.rem(m, 3) * 6 + m // 3] = packed[g]
@@ -251,6 +254,26 @@
         product(to_ref(tmp_a), perm2, got(spread))
         product(to_ref(tmp_b), perm2, got(outgrad))
         grad(n, tmp_a, tmp_b)
+
+    def grad_direct(first, second):
+        gall[...] = shares(first, second)
+
+        def step(i):
+            peer = dp_peer(i)
+            pltpu.make_async_remote_copy(
+                src_ref=gall.at[peer], dst_ref=gland.at[me_g], send_sem=dssem, recv_sem=drsem,
+                device_id={"dp": peer}, device_id_type=MESH,
+            ).start()
+
+        loop(n_dp - 1, step)
+        gland[me_g] = gall[me_g]
+
+    def direct_all():
+        return pltpu.make_async_remote_copy(
+            src_ref=gall.at[pl.ds(0, n_dp - 1)], dst_ref=gland.at[pl.ds(0, n_dp - 1)],
+            send_sem=dssem, recv_sem=drsem,
+            device_id={"dp": dp_peer(0)}, device_id_type=MESH,
+        )
 
     def finish_grad(n):
         far_all(n).wait_recv()
@@ -374,14 +397,17 @@
     product(to_send(DOWN1), mats.at[WD], plain(hidden))
     start_feat(DOWN1)
 
+    feat_all(DOWN1).wait_recv()
+    product(to_send(DOWN2), mats.at[LD], got(DOWN1))
+    start_feat(DOWN2)
     feat_all(CT).wait_recv()
     product(to_send(DSG), mats.at[LDT], got(CT))
     start_feat(DSG)
-
-    feat_all(DOWN1).wait_recv()
-    product(to_send(DOWN2), mats.at[LD], got(DOWN1))
-    start_feat(DOWN2)
     grad_left(5, DOWN1, CT)
+    feat_all(DOWN2).wait_recv()
+    to_lanes(1, pick_slots, lambda c: recv[DOWN2, pl.ds(c * 8, 8)].reshape(128, slots))
+    relay(5)
+    start_dp(1)
 
     feat_all(DSG).wait_recv()
     for s, w in tiles(slots, 128):
@@ -395,11 +421,6 @@
     product(to_ref(tmp_a), perm1, plain(hidden))
     product(to_ref(tmp_b), perm1, got(DSG))
     grad(4, tmp_a, tmp_b)
-    feat_all(DOWN2).wait_recv()
-    to_lanes(1, pick_slots, lambda c: recv[DOWN2, pl.ds(c * 8, 8)].reshape(128, slots))
-    relay(5)
-    relay(4)
-    start_dp(1)
 
     feat_all(GGRAD).wait_recv()
     product(to_send(GSG), mats.at[LGT], got(GGRAD))
@@ -413,29 +434,31 @@
     feat_all(GSG).wait_recv()
     product(to_ref(tmp_b), perm1, got(GSG))
     grad(0, mixed, tmp_b)
+    relay(4)
+    relay(1)
+    relay(3)
     feat_all(USG).wait_recv()
     product(to_ref(tmp_b), perm1, got(USG))
-    grad(2, mixed, tmp_b)
-    relay(1)
-    relay(3)
+    grad_direct(mixed, tmp_b)
     relay(0)
     for s, w in tiles(slots, 256):
         value = dot_nn(mats[WGT], flat(recv, GSG, s, w)) + dot_nn(mats[WUT], flat(recv, USG, s, w))
         mgrad_ref[:, pl.ds(s, w)] = value.astype(BF)
-    relay(2)
-
     dp_all(1).wait_recv()
     for c in range(4):
         cperm[pl.ds(c * 128, 128), :] = from_lanes(1, pick_rows, c).astype(BF)
     product(to_ref(out_ref), perm1, plain(cperm), total=rows)
 
-    for n in (5, 4, 1, 3, 0, 2):
+    for n in (5, 4, 1, 3, 0):
         finish_grad(n)
+    direct_all().wait_recv()
+    grads_ref[2] = jnp.sum(gland[...].astype(F32), axis=0) * ((rows * n_dp) ** (-0.5))
     for n in range(12):
         feat_all(n).wait_send()
     for n in range(2):
         dp_all(n).wait_send()
-    for n in range(6):
+    direct_all().wait_send()
+    for n in (0, 1, 3, 4, 5):
         near(n, 0).wait_send()
         near(n, 1).wait_send()
         far_all(n).wait_send()
@@ -481,6 +504,8 @@
             pltpu.VMEM((6, 2, 5, 32, 128), BF),
             pltpu.VMEM((6, 5, 32, 128), BF),
             pltpu.VMEM((6, 5, 32, 128), BF),
+            pltpu.VMEM((n_dp, 32, 128), BF),
+            pltpu.VMEM((n_dp, 32, 128), BF),
             pltpu.VMEM((n_dp, slots), I32),
             pltpu.VMEM((12, feats, feats), BF),
             square, square, square, square,
@@ -502,6 +527,8 @@
             pltpu.SemaphoreType.DMA((6, 2)),
             pltpu.SemaphoreType.DMA((6,)),
             pltpu.SemaphoreType.DMA((6,)),
+            pltpu.SemaphoreType.DMA,
+            pltpu.SemaphoreType.DMA,
         ],
         compiler_params=pltpu.CompilerParams(
             collective_id=0, has_side_effects=True, vmem_limit_bytes=60 << 20

time: 136 us -> 139 us (1.022)
  Pallas kernels: 135 us -> 138 us
    pallas_call x1, Pallas kernels: 133 us -> 136 us  [body(): pl.pallas_call(kernel, out_shape=packed + (jax.ShapeDtypeStruct((6, 32, 1...]
where the time goes in v3:
time: 139 us
  Pallas kernels  138 us (99%)
    pallas_call x1, Pallas kernels, body(): pl.pallas_call(kernel, out_shape=packed + (jax.ShapeDtypeStruct((6, 32, 1...  136 us

profile of v3, /device:TPU:1, one launch (start us, length us, event | category | flops | bytes accessed | tf_op | source)
XLA Modules:
  0.0 138.6 jit_solution(9586134958091003396)
XLA Ops:
  0.6 135.7 %shard_map.161 = (bf16[512,512]{1,0:T(8,128)(2,1)}, bf16[512,640]{1,0:T(8,128)(2,1)}, f32[6,32,128]{2,1,0:T(8,128)}) custom-call(f32[3]{0:T(128)} %weights_ref.1, bf16[3,512,640]{2,1,0:T(8,128)(2,1)} %earlier_in.1, s32[80,128]{1,0:T(8,128)} %bitcast.1, bf16[512,512]{1,0:T(8,128)(2,1)} %cot_in.1, bf16[4,128,128]{2,1,0:T(8,128)(2,1)} %rg_in.1, ...), custom_call_target="tpu_custom_call" | custom-call | tf_op jit(solution)/shard_map/pallas_call | solution.py:488
  136.3 2.3 %shard_map.162 = (bf16[512,512]{1,0:T(8,128)(2,1)}, bf16[512,640]{1,0:T(8,128)(2,1)}, f32[4,8,128]{2,1,0:T(8,128)}, f32[4,8,128]{2,1,0:T(8,128)}, f32[4,8,128]{2...) custom-call(bf16[512,512]{1,0:T(8,128)(2,1)} %get-tuple-element.11.out_ref, ...), custom_call_target="tpu_custom_call" | custom-call | tf_op jit(solution)/shard_map/pallas_call | solution.py:537
